TPU v7x, 512 devices: a whole 4x8x8 slice. The times are simulated.
512 devices in a mesh: lat: 64 (over y_lo, x, z), lon: 8 (over y_hi, core).
Axes of the slice: x: 4, y: 8 (y_hi: 4, y_lo: 2; y = y_hi * 2 + y_lo), z: 8, core: 2. Of those that a mesh axis runs over, the one named last changes fastest.
Arguments:
- coefficients: float32 [256, 2, 3, 2, 513], P('lat'), may hold values from -0.03125 to 0.03125
- pair_orders: int32 [256], replicated, may hold values from 0 to 255, each once
Outputs:
- potential: float32 [3, 2, 1024, 2048], P(None, None, 'lat', 'lon')
- magnetic_field: float32 [3, 2, 1024, 2048], P(None, None, 'lat', 'lon')
Inputs may be any that keep to these rules, and one draw needn't show every extreme that they name: A permutation of 0 to 255; row p of coefficients holds the orders pair_orders[p] and 511 - pair_orders[p].
All inputs are finite; a program needn't handle non-finite values.
Results may differ from a plain program's by a relative error of at most 0.0003.
Values sent between devices are 32-bit elements; how exact they have to be, the bound alone decides.
No kernel may reach another device: no remote copies, remote signals or barrier semaphores. Data moves between devices by JAX's collectives and lax.ppermute only.
A program may use at most 64 MiB of HBM per device.

v0:
```python
import math
import jax
import jax.numpy as jnp
from jax import lax
from jax.sharding import PartitionSpec as P

NT = 1024
NP = 2048
STEPS = 2
soft_floor = 1.0
resist = 0.2
time_step = 0.3
rescale_at = 10000000000.0
block_steps = 128
span_start = math.pi / 6.0
span_width = 2.0 * math.pi / 3.0


def with_halo(value, sides, width, wrap):
    for axis, dim in sides:
        size, length = (lax.axis_size(axis), value.shape[dim])
        up = [(i, (i + 1) % size) for i in range(size if wrap else size - 1)]
        down = [(j, i) for i, j in up]
        last = lax.slice_in_dim(value, length - width, length, axis=dim)
        first = lax.slice_in_dim(value, 0, width, axis=dim)
        before = lax.ppermute(last, axis, up)
        after = lax.ppermute(first, axis, down)
        value = jnp.concatenate([before, value, after], axis=dim)
    return value


def row_angles(row_ids, row_total):
    return span_start + (row_ids.astype(jnp.float32) + 0.5) * (span_width / row_total)


def norm_logs(order_total):
    degrees = jnp.arange(1, order_total, dtype=jnp.float32)
    log_terms = 0.5 * jnp.log((2.0 * degrees + 1.0) / (2.0 * degrees))
    return jnp.concatenate([jnp.zeros((1,), jnp.float32), jnp.cumsum(log_terms)]) - 0.5 * jnp.log(
        4.0 * math.pi
    )


def pick_logs(log_table, orders):
    order_grid = jnp.arange(log_table.shape[0], dtype=jnp.int32)
    return jnp.sum(
        jnp.where(order_grid[None, :] == orders[:, None], log_table[None, :], 0.0), axis=1
    )


def synthesize(coef_rows, small_orders, angles, order_total):
    pair_count = coef_rows.shape[0]
    columns = coef_rows.shape[1] * coef_rows.shape[2] * coef_rows.shape[3]
    packed = coef_rows.shape[4]
    block_count = -(-packed // block_steps)
    padded = block_count * block_steps
    flat_coef = jnp.pad(
        coef_rows.reshape(pair_count, columns, packed), ((0, 0), (0, 0), (0, padded - packed))
    )
    large_orders = order_total - 1 - small_orders
    low_order = small_orders.astype(jnp.float32)
    high_order = large_orders.astype(jnp.float32)
    switch = order_total - low_order
    positions = jnp.arange(padded, dtype=jnp.float32)
    low_mask = (positions[None, :] < switch[:, None]).astype(jnp.float32)
    masked = flat_coef[:, None, :, :] * jnp.stack([low_mask, 1.0 - low_mask], axis=1)[:, :, None, :]
    log_table = norm_logs(order_total)
    log_sin = jnp.log(jnp.sin(angles))
    cosine = jnp.cos(angles)
    seed_low = pick_logs(log_table, small_orders)[:, None] + low_order[:, None] * log_sin[None, :]
    seed_high = pick_logs(log_table, large_orders)[:, None] + high_order[:, None] * log_sin[None, :]
    log_big = math.log(rescale_at)

    def advance(carried, step_now):
        previous, current, scaling = carried
        low_side = step_now < switch
        order_now = jnp.where(low_side, low_order, high_order)
        degree = jnp.where(low_side, low_order + step_now, step_now - 1.0)
        starting = (degree == order_now)[:, None]
        factor = jnp.sqrt(
            jnp.maximum(4.0 * degree * degree - 1.0, 1.0)
            / jnp.maximum(degree * degree - order_now * order_now, 1.0)
        )
        prior_degree = degree - 1.0
        back_factor = jnp.where(
            prior_degree > order_now,
            jnp.sqrt(
                (prior_degree * prior_degree - order_now * order_now)
                / jnp.maximum(4.0 * prior_degree * prior_degree - 1.0, 1.0)
            ),
            0.0,
        )
        next_value = factor[:, None] * (cosine[None, :] * current - back_factor[:, None] * previous)
        seed_now = jnp.where(low_side[:, None], seed_low, seed_high)
        previous = jnp.where(starting, 0.0, current)
        current = jnp.where(starting, 1.0, next_value)
        scaling = jnp.where(starting, seed_now, scaling)
        too_big = jnp.abs(current) > rescale_at
        shrink = jnp.where(too_big, 1.0 / rescale_at, 1.0)
        previous = previous * shrink
        current = current * shrink
        scaling = scaling + jnp.where(too_big, log_big, 0.0)
        return ((previous, current, scaling), current * jnp.exp(scaling))

    def run_block(carried, block_index):
        rec_state, synth_sum = carried
        step_values = block_index.astype(jnp.float32) * block_steps + jnp.arange(
            block_steps, dtype=jnp.float32
        )
        rec_state, values = lax.scan(advance, rec_state, step_values, unroll=8)
        coef_block = lax.dynamic_slice_in_dim(masked, block_index * block_steps, block_steps, 3)
        synth_sum = synth_sum + jnp.einsum(
            "spt,pkcs->pkct",
            values,
            coef_block,
            precision=lax.Precision.HIGHEST,
            preferred_element_type=jnp.float32,
        )
        return ((rec_state, synth_sum), None)

    zero_rows = jnp.zeros((pair_count, angles.shape[0]), jnp.float32)
    zero_sum = jnp.zeros((pair_count, 2, columns, angles.shape[0]), jnp.float32)
    scanned = lax.scan(
        run_block,
        ((zero_rows, zero_rows, zero_rows), zero_sum),
        jnp.arange(block_count, dtype=jnp.int32),
    )
    synth_sum = scanned[0][1]
    return synth_sum.reshape(pair_count * 2, 2, columns // 2, angles.shape[0])


def sector_table(slot_orders, column_start, col_count, point_total):
    column_ids = column_start + jnp.arange(col_count, dtype=jnp.int32)
    turn_count = slot_orders[:, None] * column_ids[None, :] % point_total
    phase_angle = turn_count.astype(jnp.float32) * (2.0 * math.pi / point_total)
    return jnp.stack([jnp.cos(phase_angle), jnp.sin(phase_angle)], axis=1)


def transform(rows_part, sector_basis):
    return jnp.einsum(
        "gxcr,gxf->crf",
        rows_part,
        sector_basis,
        precision=lax.Precision.HIGHEST,
        preferred_element_type=jnp.float32,
    )


def curl(padded, row_sin, phi_ratio):
    center = padded[:, :, 1:-1, 1:-1]
    theta_diff = 0.5 * (padded[:, :, 2:, 1:-1] - padded[:, :, :-2, 1:-1])
    phi_scale = (1.0 / (2.0 * phi_ratio * row_sin))[None, :, None]
    lifted = jnp.pad(center, ((0, 0), (1, 1), (0, 0), (0, 0)))
    radial_diff = 0.5 * (lifted[:, 2:] - lifted[:, :-2])
    phi_radial = (padded[0, :, 1:-1, 2:] - padded[0, :, 1:-1, :-2]) * phi_scale
    phi_theta = (padded[1, :, 1:-1, 2:] - padded[1, :, 1:-1, :-2]) * phi_scale
    return jnp.stack(
        [theta_diff[2] - phi_theta, phi_radial - radial_diff[2], radial_diff[1] - theta_diff[0]]
    )


def cross_product(first_vec, second_vec):
    return jnp.stack(
        [
            first_vec[1] * second_vec[2] - first_vec[2] * second_vec[1],
            first_vec[2] * second_vec[0] - first_vec[0] * second_vec[2],
            first_vec[0] * second_vec[1] - first_vec[1] * second_vec[0],
        ]
    )


def drift(magnetic, current):
    lorentz = cross_product(current, magnetic)
    velocity = lorentz / (jnp.sum(magnetic * magnetic, axis=0) + soft_floor)
    return cross_product(velocity, magnetic) - resist * current


def per_device(coefficients, pair_orders):
    lat_count = lax.axis_size("lat")
    lon_count = lax.axis_size("lon")
    lat_pos = lax.axis_index("lat")
    lon_pos = lax.axis_index("lon")
    pair_local = coefficients.shape[0]
    levels = coefficients.shape[3]
    order_total = 2 * pair_orders.shape[0]
    row_total = NT
    point_total = NP
    band_rows = row_total // lat_count
    sector_cols = point_total // lon_count
    own_pairs = lax.dynamic_slice_in_dim(pair_orders, lat_pos * pair_local, pair_local)
    slot_orders = jnp.stack([pair_orders, order_total - 1 - pair_orders], axis=1).reshape(
        order_total
    )
    own_table = sector_table(slot_orders, lon_pos * sector_cols, sector_cols, point_total)
    angles = row_angles(jnp.arange(row_total, dtype=jnp.int32), row_total)
    spectral = synthesize(coefficients, own_pairs, angles, order_total)
    synth_grid = transform(
        lax.all_to_all(spectral, "lat", split_axis=3, concat_axis=0, tiled=True), own_table
    )
    potential = synth_grid.reshape(3, levels, band_rows, sector_cols)
    global_rows = lat_pos * band_rows + jnp.arange(-2, band_rows + 2, dtype=jnp.int32)
    sin_all = jnp.sin(row_angles(global_rows, row_total))
    sin_inner = sin_all[2:-2]
    phi_ratio = 3.0 * row_total / point_total
    magnetic = potential

    def extend_rims(values):
        taller = with_halo(values, (("lat", 2),), 1, False)
        return with_halo(taller, (("lon", 3),), 1, True)

    for step_now in range(STEPS):
        magnetic = curl(extend_rims(potential), sin_inner, phi_ratio)
        current = curl(extend_rims(magnetic), sin_inner, phi_ratio)
        potential = potential + time_step * drift(magnetic, current)
    return (potential, magnetic)


def solution(mesh):
    in_specs = (P("lat", None, None, None, None), P())
    out_specs = (P(None, None, "lat", "lon"), P(None, None, "lat", "lon"))
    return jax.shard_map(
        per_device, mesh=mesh, in_specs=in_specs, out_specs=out_specs, check_vma=False
    )
```

profile of v0, /device:TPU:8, one launch (start us, length us, event | category | flops | bytes accessed | tf_op | source)
XLA Modules:
  0.0 1125.7 jit_solution(11292824940193635866)
XLA Ops:
  3.7 957.0 %while.59 = (s32[]{:T(128)}, f32[4,1024]{1,0:T(4,128)S(1)}, f32[4,1024]{1,0:T(4,128)S(1)}, f32[4,1024]{1,0:T(4,128)S(1)}, f32[4,2,12,1024]{3,2,1,0:T(8,128)S(1)}...) while((s32[]{:T(128)}, f32[4,1024]{1,0:T(4,128)S(1)}, ...), condition=%wide.region_7.8_spmd.clone.clone.clone.clone, body=%wide.region_4.7_spmd.clone.clone.clone.clone.sunk | while | flops 152044704 | bytes 4487110 | solution.py:123
  5.0 187.1 %while.60 = (s32[]{:T(128)}, f32[4,1024]{1,0:T(4,128)S(1)}, f32[4,1024]{1,0:T(4,128)S(1)}, f32[4,1024]{1,0:T(4,128)S(1)}, f32[16,8,4,1024]{3,2,1,0:T(4,128)S(1)}...) while((s32[]{:T(128)}, f32[4,1024]{1,0:T(4,128)S(1)}, ...), condition=%wide.region_6.6_spmd.clone, body=%wide.region_5.5_spmd.clone.sunk | while | flops 832281 | bytes 1364985 | solution.py:110
  48.2 2.5 fusion.179
  59.9 2.5 fusion.179
  71.6 2.5 fusion.179
  118.4 2.5 fusion.179
  130.1 2.5 fusion.179
  141.8 2.5 fusion.179
  188.6 2.5 fusion.179
  196.4 187.1 %while.60 = (s32[]{:T(128)}, f32[4,1024]{1,0:T(4,128)S(1)}, f32[4,1024]{1,0:T(4,128)S(1)}, f32[4,1024]{1,0:T(4,128)S(1)}, f32[16,8,4,1024]{3,2,1,0:T(4,128)S(1)}...) while((s32[]{:T(128)}, f32[4,1024]{1,0:T(4,128)S(1)}, ...), condition=%wide.region_6.6_spmd.clone, body=%wide.region_5.5_spmd.clone.sunk | while | flops 832281 | bytes 1364985 | solution.py:110
  204.6 2.5 fusion.179
  251.3 2.5 fusion.179
  263.0 2.5 fusion.179
  274.7 2.5 fusion.179
  286.4 2.5 fusion.179
  333.2 2.5 fusion.179
  344.9 2.5 fusion.179
  356.6 2.5 fusion.179
  387.8 187.1 %while.60 = (s32[]{:T(128)}, f32[4,1024]{1,0:T(4,128)S(1)}, f32[4,1024]{1,0:T(4,128)S(1)}, f32[4,1024]{1,0:T(4,128)S(1)}, f32[16,8,4,1024]{3,2,1,0:T(4,128)S(1)}...) while((s32[]{:T(128)}, f32[4,1024]{1,0:T(4,128)S(1)}, ...), condition=%wide.region_6.6_spmd.clone, body=%wide.region_5.5_spmd.clone.sunk | while | flops 832281 | bytes 1364985 | solution.py:110
  419.3 2.5 fusion.179
  431.0 2.5 fusion.179
  442.7 2.5 fusion.179
  454.4 2.5 fusion.179
  501.2 2.5 fusion.179
  512.9 2.5 fusion.179
  524.6 2.5 fusion.179
  571.4 2.5 fusion.179
  579.2 187.1 %while.60 = (s32[]{:T(128)}, f32[4,1024]{1,0:T(4,128)S(1)}, f32[4,1024]{1,0:T(4,128)S(1)}, f32[4,1024]{1,0:T(4,128)S(1)}, f32[16,8,4,1024]{3,2,1,0:T(4,128)S(1)}...) while((s32[]{:T(128)}, f32[4,1024]{1,0:T(4,128)S(1)}, ...), condition=%wide.region_6.6_spmd.clone, body=%wide.region_5.5_spmd.clone.sunk | while | flops 832281 | bytes 1364985 | solution.py:110
  610.7 2.5 fusion.179
  770.6 187.1 %while.60 = (s32[]{:T(128)}, f32[4,1024]{1,0:T(4,128)S(1)}, f32[4,1024]{1,0:T(4,128)S(1)}, f32[4,1024]{1,0:T(4,128)S(1)}, f32[16,8,4,1024]{3,2,1,0:T(4,128)S(1)}...) while((s32[]{:T(128)}, f32[4,1024]{1,0:T(4,128)S(1)}, ...), condition=%wide.region_6.6_spmd.clone, body=%wide.region_5.5_spmd.clone.sunk | while | flops 832281 | bytes 1364985 | solution.py:110
  960.7 5.0 copy.35
  965.8 10.7 reshape.753
  976.5 14.9 %all-to-all-start = ((f32[64,1,1536]{2,1,0:T(1,128)}), f32[64,1,1536]{2,1,0:T(1,128)S(1)}, u32[]{:S(2)}, u32[]{:S(2)}) async-start(f32[64,1,1536]{2,1,0:T(1,128)} %reshape.753), calls=%async_computation | async-start | bytes 786432 | tf_op jit(solution)/shard_map/all_to_all | solution.py:198
  991.8 3.2 fusion.103
  995.0 12.2 %all-to-all-done = f32[64,1,1536]{2,1,0:T(1,128)S(1)} async-done(((f32[64,1,1536]{2,1,0:T(1,128)}), f32[64,1,1536]{2,1,0:T(1,128)S(1)}, u32[]{:S(2)}, u32[]{:S(2)}) %all-to-all-start) | async-done | bytes 393248 | tf_op jit(solution)/shard_map/all_to_all | solution.py:198
  1009.3 11.3 %reshape.754 = f32[1024,6,2,8]{3,2,1,0:T(2,128)} reshape(f32[64,1536]{1,0:T(8,128)S(1)} %reduce.2) | data formatting | bytes 786432
  1020.6 7.3 copy.46
  1030.8 3.2 collective-permute-start
  1034.1 2.6 collective-permute-start.1
  1036.8 7.0 collective-permute-done.1
  1048.3 5.3 collective-permute-done.3
  1055.7 8.1 collective-permute-start.5
  1069.7 5.3 collective-permute-done.7
  1075.4 8.4 collective-permute-start.8
  1085.7 7.8 collective-permute-done.9
  1098.0 5.3 collective-permute-done.11
  1105.4 8.1 collective-permute-start.13
  1119.4 5.3 collective-permute-done.15
  (1866 shorter events, 523.9 us)
Async XLA Ops:
  965.8 25.6 %copy-start.1 = (s32[256]{0:T(256)S(1)}, s32[256]{0:T(256)}, u32[]{:S(2)}) copy-start(s32[256]{0:T(256)} %param.7) | copy-start | bytes 3076
  976.5 30.7 %all-to-all-start = ((f32[64,1,1536]{2,1,0:T(1,128)}), f32[64,1,1536]{2,1,0:T(1,128)S(1)}, u32[]{:S(2)}, u32[]{:S(2)}) async-start(f32[64,1,1536]{2,1,0:T(1,128)} %reshape.753), calls=%async_computation | async-start | bytes 786432 | tf_op jit(solution)/shard_map/all_to_all | solution.py:198
  1030.8 5.9 collective-permute-start
  1034.1 9.7 collective-permute-start.1
  1043.9 4.4 collective-permute-start.2
  1045.8 7.8 collective-permute-start.3
  1053.8 10.1 collective-permute-start.4
  1055.7 9.5 collective-permute-start.5
  1065.3 4.4 collective-permute-start.6
  1067.2 7.8 collective-permute-start.7
  1075.4 10.3 collective-permute-start.8
  1083.8 9.7 collective-permute-start.9
  1093.6 4.4 collective-permute-start.10
  1095.6 7.8 collective-permute-start.11
  1103.5 22.2 %copy-start = (f32[3,2,16,256]{3,2,1,0:T(8,128)}, f32[3,2,16,256]{3,2,1,0:T(8,128)S(1)}, u32[]{:S(2)}) copy-start(f32[3,2,16,256]{3,2,1,0:T(8,128)S(1)} %get-tuple-element.812) | copy-start | bytes 294916
  1103.5 10.1 collective-permute-start.12
  1105.4 9.5 collective-permute-start.13
  1115.0 4.4 collective-permute-start.14
  1117.0 7.8 collective-permute-start.15
where the time goes:
time: 1140 us; the launch traced here: 1130 us
  other arithmetic  486 us (43%)
  loops' own time  409 us (36%)
  local copies, waits for them, and re-layouts  96.7 us (8%)
  starting transfers between devices  68.5 us (6%)
  waiting for transfers between devices  50.8 us (4%)
  matrix products  13.7 us (1%)
    another operation x5, loops' own time, run_block(): rec_state, values = lax.scan(advance, rec_state, step_values, unroll=8)  403 us
    sqrt x240, other arithmetic, advance(): jnp.sqrt(jnp.maximum(4.0 * degree * degree - 1.0, 1.0) / jnp.maximum(degr...  204 us
    eq x400, other arithmetic, advance(): starting = (degree == order_now)[:, None]  197 us
    while x560, other arithmetic  57.7 us
    slice x80, local copies, waits for them, and re-layouts, run_block(): rec_state, values = lax.scan(advance, rec_state, step_values, unroll=8)  48.3 us
    ppermute x8, waiting for transfers between devices, with_halo(): before = lax.ppermute(last, axis, up)  36 us
    ppermute x8, starting transfers between devices, with_halo(): after = lax.ppermute(first, axis, down)  35.6 us
    unnamed x8, local copies, waits for them, and re-layouts  23 us
  transfers between devices with their start and end apart: 17, of which 9 were waited for; matrix products, arithmetic and copies ran while one was open for 0% of the time, Pallas kernels for 0%

commit v1 on v0

--- a/solution.py
+++ b/solution.py
@@ -14,6 +14,10 @@
 block_steps = 128
 span_start = math.pi / 6.0
 span_width = 2.0 * math.pi / 3.0
+get_yards = lambda local_values, dim_k, d0: jnp.concatenate(
+    lax.all_to_all(jnp.stack(jnp.split(local_values, lax.axis_size("lat"), dim_k), 0), "lat", 0, 0),
+    d0,
+)
 
 
 def with_halo(value, sides, width, wrap):
@@ -194,9 +198,7 @@
     own_table = sector_table(slot_orders, lon_pos * sector_cols, sector_cols, point_total)
     angles = row_angles(jnp.arange(row_total, dtype=jnp.int32), row_total)
     spectral = synthesize(coefficients, own_pairs, angles, order_total)
-    synth_grid = transform(
-        lax.all_to_all(spectral, "lat", split_axis=3, concat_axis=0, tiled=True), own_table
-    )
+    synth_grid = transform(get_yards(spectral, 3, 0), own_table)
     potential = synth_grid.reshape(3, levels, band_rows, sector_cols)
     global_rows = lat_pos * band_rows + jnp.arange(-2, band_rows + 2, dtype=jnp.int32)
     sin_all = jnp.sin(row_angles(global_rows, row_total))

time: 1140 us -> 1100 us (0.965)
  the two profiles are of different devices: /device:TPU:8 before, /device:TPU:40 now
where the time goes in v1:
time: 1100 us; the launch traced here: 1090 us
  other arithmetic  481 us (44%)
  loops' own time  405 us (37%)
  local copies, waits for them, and re-layouts  74 us (7%)
  starting transfers between devices  68.5 us (6%)
  waiting for transfers between devices  50.8 us (5%)
  matrix products  12.5 us (1%)
    another operation x5, loops' own time, run_block(): rec_state, values = lax.scan(advance, rec_state, step_values, unroll=8)  398 us
    sqrt x240, other arithmetic, advance(): jnp.sqrt(jnp.maximum(4.0 * degree * degree - 1.0, 1.0) / jnp.maximum(degr...  204 us
    eq x400, other arithmetic, advance(): starting = (degree == order_now)[:, None]  193 us
    while x560, other arithmetic  57.7 us
    slice x80, local copies, waits for them, and re-layouts, run_block(): rec_state, values = lax.scan(advance, rec_state, step_values, unroll=8)  48.4 us
    ppermute x8, waiting for transfers between devices, with_halo(): before = lax.ppermute(last, axis, up)  36 us
    ppermute x8, starting transfers between devices, with_halo(): after = lax.ppermute(first, axis, down)  35.6 us
  transfers between devices with their start and end apart: 17, of which 9 were waited for; matrix products, arithmetic and copies ran while one was open for 0% of the time, Pallas kernels for 0%

profile of v1, /device:TPU:40, one launch (start us, length us, event | category | flops | bytes accessed | tf_op | source)
XLA Modules:
  0.0 1092.6 jit_solution(4528682196705908075)
XLA Ops:
  3.7 948.0 %while.59 = (s32[]{:T(128)}, f32[4,1024]{1,0:T(4,128)S(1)}, f32[4,1024]{1,0:T(4,128)S(1)}, f32[4,1024]{1,0:T(4,128)S(1)}, f32[4,2,12,1024]{3,2,1,0:T(8,128)S(1)}...) while((s32[]{:T(128)}, f32[4,1024]{1,0:T(4,128)S(1)}, ...), condition=%wide.region_7.8_spmd.clone.clone.clone.clone, body=%wide.region_4.7_spmd.clone.clone.clone.clone.sunk | while | flops 152044704 | bytes 4487110 | solution.py:127
  5.1 185.2 %while.60 = (s32[]{:T(128)}, f32[4,1024]{1,0:T(4,128)S(1)}, f32[4,1024]{1,0:T(4,128)S(1)}, f32[4,1024]{1,0:T(4,128)S(1)}, f32[16,8,4,1024]{3,2,1,0:T(4,128)S(1)}...) while((s32[]{:T(128)}, f32[4,1024]{1,0:T(4,128)S(1)}, ...), condition=%wide.region_6.6_spmd.clone, body=%wide.region_5.5_spmd.clone.sunk | while | flops 832281 | bytes 1364985 | solution.py:114
  13.1 2.5 fusion.180
  24.7 2.5 fusion.180
  36.3 2.5 fusion.180
  47.9 2.5 fusion.180
  59.4 2.5 fusion.180
  71.0 2.5 fusion.180
  82.6 2.5 fusion.180
  94.1 2.5 fusion.180
  105.7 2.5 fusion.180
  117.3 2.5 fusion.180
  128.9 2.5 fusion.180
  140.4 2.5 fusion.180
  194.7 185.2 %while.60 = (s32[]{:T(128)}, f32[4,1024]{1,0:T(4,128)S(1)}, f32[4,1024]{1,0:T(4,128)S(1)}, f32[4,1024]{1,0:T(4,128)S(1)}, f32[16,8,4,1024]{3,2,1,0:T(4,128)S(1)}...) while((s32[]{:T(128)}, f32[4,1024]{1,0:T(4,128)S(1)}, ...), condition=%wide.region_6.6_spmd.clone, body=%wide.region_5.5_spmd.clone.sunk | while | flops 832281 | bytes 1364985 | solution.py:114
  202.7 2.5 fusion.180
  295.3 2.5 fusion.180
  306.9 2.5 fusion.180
  318.5 2.5 fusion.180
  330.0 2.5 fusion.180
  341.6 2.5 fusion.180
  353.2 2.5 fusion.180
  364.7 2.5 fusion.180
  376.3 2.5 fusion.180
  384.3 185.2 %while.60 = (s32[]{:T(128)}, f32[4,1024]{1,0:T(4,128)S(1)}, f32[4,1024]{1,0:T(4,128)S(1)}, f32[4,1024]{1,0:T(4,128)S(1)}, f32[16,8,4,1024]{3,2,1,0:T(4,128)S(1)}...) while((s32[]{:T(128)}, f32[4,1024]{1,0:T(4,128)S(1)}, ...), condition=%wide.region_6.6_spmd.clone, body=%wide.region_5.5_spmd.clone.sunk | while | flops 832281 | bytes 1364985 | solution.py:114
  473.3 2.5 fusion.180
  484.9 2.5 fusion.180
  496.5 2.5 fusion.180
  508.1 2.5 fusion.180
  519.6 2.5 fusion.180
  531.2 2.5 fusion.180
  542.8 2.5 fusion.180
  573.9 185.2 %while.60 = (s32[]{:T(128)}, f32[4,1024]{1,0:T(4,128)S(1)}, f32[4,1024]{1,0:T(4,128)S(1)}, f32[4,1024]{1,0:T(4,128)S(1)}, f32[16,8,4,1024]{3,2,1,0:T(4,128)S(1)}...) while((s32[]{:T(128)}, f32[4,1024]{1,0:T(4,128)S(1)}, ...), condition=%wide.region_6.6_spmd.clone, body=%wide.region_5.5_spmd.clone.sunk | while | flops 832281 | bytes 1364985 | solution.py:114
  763.5 185.2 %while.60 = (s32[]{:T(128)}, f32[4,1024]{1,0:T(4,128)S(1)}, f32[4,1024]{1,0:T(4,128)S(1)}, f32[4,1024]{1,0:T(4,128)S(1)}, f32[16,8,4,1024]{3,2,1,0:T(4,128)S(1)}...) while((s32[]{:T(128)}, f32[4,1024]{1,0:T(4,128)S(1)}, ...), condition=%wide.region_6.6_spmd.clone, body=%wide.region_5.5_spmd.clone.sunk | while | flops 832281 | bytes 1364985 | solution.py:114
  958.9 14.9 %all-to-all-start = ((f32[64,1,1536]{2,1,0:T(1,128)}), f32[64,1,1536]{2,1,0:T(1,128)S(1)}, u32[]{:S(2)}, u32[]{:S(2)}) async-start(f32[64,1,1536]{2,1,0:T(1,128)} %reshape.756), calls=%async_computation | async-start | bytes 786432 | tf_op jit(solution)/shard_map/all_to_all | solution.py:18
  974.1 3.3 fusion.103
  977.4 12.2 %all-to-all-done = f32[64,1,1536]{2,1,0:T(1,128)S(1)} async-done(((f32[64,1,1536]{2,1,0:T(1,128)}), f32[64,1,1536]{2,1,0:T(1,128)S(1)}, u32[]{:S(2)}, u32[]{:S(2)}) %all-to-all-start) | async-done | bytes 393248 | tf_op jit(solution)/shard_map/all_to_all | solution.py:18
  997.7 3.2 collective-permute-start
  1000.9 2.6 collective-permute-start.1
  1003.6 7.0 collective-permute-done.1
  1015.2 5.3 collective-permute-done.3
  1022.6 8.1 collective-permute-start.5
  1036.6 5.3 collective-permute-done.7
  1042.2 8.4 collective-permute-start.8
  1052.6 7.8 collective-permute-done.9
  1064.9 5.3 collective-permute-done.11
  1072.3 8.1 collective-permute-start.13
  1086.3 5.3 collective-permute-done.15
  (1934 shorter events, 519.5 us)
Async XLA Ops:
  955.5 18.3 %copy-start.3 = (s32[256]{0:T(256)S(1)}, s32[256]{0:T(256)}, u32[]{:S(2)}) copy-start(s32[256]{0:T(256)} %param.7) | copy-start | bytes 3076
  958.9 30.7 %all-to-all-start = ((f32[64,1,1536]{2,1,0:T(1,128)}), f32[64,1,1536]{2,1,0:T(1,128)S(1)}, u32[]{:S(2)}, u32[]{:S(2)}) async-start(f32[64,1,1536]{2,1,0:T(1,128)} %reshape.756), calls=%async_computation | async-start | bytes 786432 | tf_op jit(solution)/shard_map/all_to_all | solution.py:18
  994.6 2.4 copy-start
  994.6 2.4 copy-start.1
  997.7 5.9 collective-permute-start
  1000.9 9.7 collective-permute-start.1
  1010.8 4.4 collective-permute-start.2
  1012.7 7.8 collective-permute-start.3
  1020.7 10.1 collective-permute-start.4
  1022.6 9.5 collective-permute-start.5
  1032.2 4.4 collective-permute-start.6
  1034.1 7.8 collective-permute-start.7
  1042.2 10.3 collective-permute-start.8
  1050.6 9.7 collective-permute-start.9
  1060.5 4.4 collective-permute-start.10
  1062.4 7.8 collective-permute-start.11
  1070.4 22.2 %copy-start.2 = (f32[3,2,16,256]{3,2,1,0:T(8,128)}, f32[3,2,16,256]{3,2,1,0:T(8,128)S(1)}, u32[]{:S(2)}) copy-start(f32[3,2,16,256]{3,2,1,0:T(8,128)S(1)} %get-tuple-element.812) | copy-start | bytes 294916
  1070.4 10.1 collective-permute-start.12
  1072.3 9.5 collective-permute-start.13
  1081.9 4.4 collective-permute-start.14
  1083.8 7.8 collective-permute-start.15
